TPU v7x, 32 devices: a whole 2x2x4 slice. The times are simulated.
32 devices in a mesh: dp: 8 (over z, y), mp: 4 (over x, core).
Axes of the slice: x: 2, y: 2, z: 4, core: 2. Of those that a mesh axis runs over, the one named last changes fastest.
Arguments:
- tokens: bfloat16 [14592, 768], P(('dp', 'mp')), may hold values from -6 to 6
- caption_mask: int32 [64, 128], P('dp'), may hold values from 0 to 1, as said below
- region_counts: int32 [16], replicated, may hold values from 36 to 100, as said below
- group_ids: int32 [64], P('dp'), may hold values from 0 to 15, as said below
- query_weight: bfloat16 [768, 768], P(None, 'mp'), may hold values from -0.21875 to 0.21875
- query_bias: float32 [768], P('mp'), may hold values from -3 to 3
- key_weight: bfloat16 [768, 768], P(None, 'mp'), may hold values from -0.21875 to 0.21875
- value_weight: bfloat16 [768, 768], P(None, 'mp'), may hold values from -0.21875 to 0.21875
- value_bias: float32 [768], P('mp'), may hold values from -3 to 3
- out_weight: bfloat16 [768, 768], P('mp'), may hold values from -1.25 to 1.25
- out_bias: float32 [768], replicated, may hold values from -3 to 3
- attn_gain: float32 [768], replicated, may hold values from 0.5 to 1.5
- attn_shift: float32 [768], replicated, may hold values from -3 to 3
- up_weight: bfloat16 [768, 3072], P(None, 'mp'), may hold values from -0.21875 to 0.21875
- up_bias: float32 [3072], P('mp'), may hold values from -3 to 3
- down_weight: bfloat16 [3072, 768], P('mp'), may hold values from -0.109375 to 0.109375
- down_bias: float32 [768], replicated, may hold values from -3 to 3
- final_gain: float32 [768], replicated, may hold values from 0.5 to 1.5
- final_shift: float32 [768], replicated, may hold values from -3 to 3
- cotangent: bfloat16 [14592, 768], P(('dp', 'mp')), may hold values from -6 to 6
Outputs:
- layer_out: bfloat16 [14592, 768], P(('dp', 'mp'))
- grad_tokens: float32 [14592, 768], P(('dp', 'mp'))
- grad_query_weight: float32 [768, 768], P(None, 'mp')
- grad_query_bias: float32 [768], P('mp')
- grad_key_weight: float32 [768, 768], P(None, 'mp')
- grad_value_weight: float32 [768, 768], P(None, 'mp')
- grad_value_bias: float32 [768], P('mp')
- grad_out_weight: float32 [768, 768], P('mp')
- grad_out_bias: float32 [768], replicated
- grad_attn_gain: float32 [768], replicated
- grad_attn_shift: float32 [768], replicated
- grad_up_weight: float32 [768, 3072], P(None, 'mp')
- grad_up_bias: float32 [3072], P('mp')
- grad_down_weight: float32 [3072, 768], P('mp')
- grad_down_bias: float32 [768], replicated
- grad_final_gain: float32 [768], replicated
- grad_final_shift: float32 [768], replicated
Inputs may be any that keep to these rules, and one draw needn't show every extreme that they name: `caption_mask`: each row is ones followed by zeros, with at least one one; some row is all ones. `region_counts`: some image has exactly 100 regions. `group_ids`: each image is named by exactly 4 sequences.
All inputs are finite; a program needn't handle non-finite values.
Results may differ from a plain program's by a relative error of at most 0.015.
Values may be sent and summed in bfloat16 or wider, within the bound.
A program may use at most 128 MiB of HBM per device.

v0:
```python
import jax
import jax.numpy as jnp
from jax import lax
from jax.sharding import PartitionSpec as P

HEAD = 64
MAXREG = 100
EPS = 1e-12
ROOT_HALF = 0.7071067811865476
DENSITY = 0.3989422804014327
MASKED = -1e30


def key_valid(caption_mask, region_counts, group_ids):
    images = region_counts.shape[0]
    match = group_ids[:, None] == jnp.arange(images, dtype=jnp.int32)[None, :]
    regions = jnp.sum(jnp.where(match, region_counts[None, :], 0), axis=1)
    slots = jnp.arange(MAXREG, dtype=jnp.int32)
    return jnp.concatenate([caption_mask > 0, slots[None, :] < regions[:, None]], axis=1)


def norm_forward(total, gain, shift):
    mean = jnp.mean(total, axis=-1, keepdims=True)
    centered = total - mean
    inverse = lax.rsqrt(jnp.mean(centered * centered, axis=-1, keepdims=True) + EPS)
    scaled = centered * inverse
    return (scaled * gain + shift, scaled, inverse)


def norm_backward(grad, scaled, inverse, gain):
    weighted = grad * gain
    centered = weighted - jnp.mean(weighted, axis=-1, keepdims=True)
    return inverse * (centered - scaled * jnp.mean(weighted * scaled, axis=-1, keepdims=True))


def split_heads(block, seqs):
    return block.reshape(seqs, -1, block.shape[1] // HEAD, HEAD)


def masked_scores(query_heads, key_heads, valid):
    scores = jnp.einsum(
        "sqhd,skhd->shqk", query_heads, key_heads, preferred_element_type=jnp.float32
    ) * HEAD ** (-0.5)
    return jnp.where(valid[:, None, None, :], scores, MASKED)


def attend(query, keys, values, valid):
    seqs = valid.shape[0]
    value_heads = split_heads(values, seqs)
    scores = masked_scores(split_heads(query, seqs), split_heads(keys, seqs), valid)
    top = jnp.max(scores, axis=-1, keepdims=True)
    weights = jnp.exp(scores - top)
    total = jnp.sum(weights, axis=-1, keepdims=True)
    probs = (weights / total).astype(jnp.bfloat16)
    context = jnp.einsum("shqk,skhd->sqhd", probs, value_heads, preferred_element_type=jnp.float32)
    return (context.reshape(query.shape).astype(jnp.bfloat16), top + jnp.log(total))


def attend_backward(query, keys, values, valid, log_total, grad_context):
    seqs = valid.shape[0]
    query_heads = split_heads(query, seqs)
    key_heads = split_heads(keys, seqs)
    value_heads = split_heads(values, seqs)
    grad_heads = split_heads(grad_context, seqs)
    probs = jnp.exp(masked_scores(query_heads, key_heads, valid) - log_total)
    grad_values = jnp.einsum(
        "shqk,sqhd->skhd",
        probs.astype(jnp.bfloat16),
        grad_heads,
        preferred_element_type=jnp.float32,
    )
    grad_probs = jnp.einsum(
        "sqhd,skhd->shqk", grad_heads, value_heads, preferred_element_type=jnp.float32
    )
    row_total = jnp.sum(probs * grad_probs, axis=-1, keepdims=True)
    grad_scores = (probs * (grad_probs - row_total)).astype(jnp.bfloat16)
    scale = HEAD ** (-0.5)
    grad_query = (
        jnp.einsum("shqk,skhd->sqhd", grad_scores, key_heads, preferred_element_type=jnp.float32)
        * scale
    )
    grad_keys = (
        jnp.einsum("shqk,sqhd->skhd", grad_scores, query_heads, preferred_element_type=jnp.float32)
        * scale
    )
    shape = query.shape
    return (
        grad_query.reshape(shape).astype(jnp.bfloat16),
        grad_keys.reshape(shape).astype(jnp.bfloat16),
        grad_values.reshape(shape).astype(jnp.bfloat16),
    )


def attention_forward(
    tokens,
    valid,
    query_weight,
    query_bias,
    key_weight,
    value_weight,
    value_bias,
    out_weight,
    out_bias,
    attn_gain,
    attn_shift,
):
    whole = lax.all_gather(tokens, "mp", axis=0, tiled=True)
    query = (jnp.dot(whole, query_weight, preferred_element_type=jnp.float32) + query_bias).astype(
        jnp.bfloat16
    )
    keys = jnp.dot(whole, key_weight, preferred_element_type=jnp.float32).astype(jnp.bfloat16)
    values = (jnp.dot(whole, value_weight, preferred_element_type=jnp.float32) + value_bias).astype(
        jnp.bfloat16
    )
    context, log_total = attend(query, keys, values, valid)
    branch = lax.psum_scatter(
        jnp.dot(context, out_weight, preferred_element_type=jnp.float32),
        "mp",
        scatter_dimension=0,
        tiled=True,
    )
    normed, scaled, inverse = norm_forward(
        tokens.astype(jnp.float32) + branch + out_bias, attn_gain, attn_shift
    )
    return (whole, query, keys, values, context, log_total, normed, scaled, inverse)


def feedforward(normed, up_weight, up_bias, down_weight, down_bias, final_gain, final_shift):
    spread = lax.all_gather(normed.astype(jnp.bfloat16), "mp", axis=0, tiled=True)
    act_in = jnp.dot(spread, up_weight, preferred_element_type=jnp.float32) + up_bias
    cdf = 0.5 * (1.0 + jax.scipy.special.erf(act_in * ROOT_HALF))
    act = (act_in * cdf).astype(jnp.bfloat16)
    second = lax.psum_scatter(
        jnp.dot(act, down_weight, preferred_element_type=jnp.float32),
        "mp",
        scatter_dimension=0,
        tiled=True,
    )
    result, scaled, inverse = norm_forward(normed + second + down_bias, final_gain, final_shift)
    return (spread, act_in, act, result, scaled, inverse)


def body(
    tokens,
    caption_mask,
    region_counts,
    group_ids,
    query_weight,
    query_bias,
    key_weight,
    value_weight,
    value_bias,
    out_weight,
    out_bias,
    attn_gain,
    attn_shift,
    up_weight,
    up_bias,
    down_weight,
    down_bias,
    final_gain,
    final_shift,
    cotangent,
):
    valid = key_valid(caption_mask, region_counts, group_ids)
    first = attention_forward(
        tokens,
        valid,
        query_weight,
        query_bias,
        key_weight,
        value_weight,
        value_bias,
        out_weight,
        out_bias,
        attn_gain,
        attn_shift,
    )
    normed = first[6]
    second = feedforward(
        normed, up_weight, up_bias, down_weight, down_bias, final_gain, final_shift
    )
    layer_out = second[3].astype(jnp.bfloat16)
    second = feedforward(
        normed, up_weight, up_bias, down_weight, down_bias, final_gain, final_shift
    )
    spread, act_in, act, unused, scaled_out, inverse_out = second
    grad_out = cotangent.astype(jnp.float32)
    grad_final = norm_backward(grad_out, scaled_out, inverse_out, final_gain)
    final_gain_part = jnp.sum(grad_out * scaled_out, axis=0)
    final_shift_part = jnp.sum(grad_out, axis=0)
    grad_branch = lax.all_gather(grad_final.astype(jnp.bfloat16), "mp", axis=0, tiled=True)
    grad_down_weight = jnp.einsum("rf,rd->fd", act, grad_branch, preferred_element_type=jnp.float32)
    grad_down_bias = jnp.sum(grad_branch, axis=0, dtype=jnp.float32)
    grad_act = jnp.einsum("rd,fd->rf", grad_branch, down_weight, preferred_element_type=jnp.float32)
    cdf = 0.5 * (1.0 + jax.scipy.special.erf(act_in * ROOT_HALF))
    slope = cdf + act_in * jnp.exp(-0.5 * act_in * act_in) * DENSITY
    grad_in = (grad_act * slope).astype(jnp.bfloat16)
    grad_up_weight = jnp.einsum("rd,rf->df", spread, grad_in, preferred_element_type=jnp.float32)
    grad_up_bias = jnp.sum(grad_in, axis=0, dtype=jnp.float32)
    grad_mid = grad_final + lax.psum_scatter(
        jnp.einsum("rf,df->rd", grad_in, up_weight, preferred_element_type=jnp.float32),
        "mp",
        scatter_dimension=0,
        tiled=True,
    )
    upper_grads = (grad_up_weight, grad_up_bias, grad_down_weight, grad_down_bias)
    first = attention_forward(
        tokens,
        valid,
        query_weight,
        query_bias,
        key_weight,
        value_weight,
        value_bias,
        out_weight,
        out_bias,
        attn_gain,
        attn_shift,
    )
    whole, query, keys, values, context, log_total, unused_mid, scaled_mid, inverse_mid = first
    grad_first = norm_backward(grad_mid, scaled_mid, inverse_mid, attn_gain)
    attn_gain_part = jnp.sum(grad_mid * scaled_mid, axis=0)
    attn_shift_part = jnp.sum(grad_mid, axis=0)
    grad_attn = lax.all_gather(grad_first.astype(jnp.bfloat16), "mp", axis=0, tiled=True)
    grad_out_weight = jnp.einsum(
        "rc,rd->cd", context, grad_attn, preferred_element_type=jnp.float32
    )
    grad_out_bias = jnp.sum(grad_attn, axis=0, dtype=jnp.float32)
    grad_context = jnp.einsum(
        "rd,cd->rc", grad_attn, out_weight, preferred_element_type=jnp.float32
    ).astype(jnp.bfloat16)
    grad_query, grad_keys, grad_values = attend_backward(
        query, keys, values, valid, log_total, grad_context
    )
    grad_query_weight = jnp.einsum(
        "rd,rc->dc", whole, grad_query, preferred_element_type=jnp.float32
    )
    grad_query_bias = jnp.sum(grad_query, axis=0, dtype=jnp.float32)
    grad_key_weight = jnp.einsum("rd,rc->dc", whole, grad_keys, preferred_element_type=jnp.float32)
    grad_value_weight = jnp.einsum(
        "rd,rc->dc", whole, grad_values, preferred_element_type=jnp.float32
    )
    grad_value_bias = jnp.sum(grad_values, axis=0, dtype=jnp.float32)
    total = jnp.einsum("rc,dc->rd", grad_query, query_weight, preferred_element_type=jnp.float32)
    total = total + jnp.einsum(
        "rc,dc->rd", grad_keys, key_weight, preferred_element_type=jnp.float32
    )
    grad_tokens = grad_first + lax.psum_scatter(
        (
            total
            + jnp.einsum("rc,dc->rd", grad_values, value_weight, preferred_element_type=jnp.float32)
        ).astype(jnp.bfloat16),
        "mp",
        scatter_dimension=0,
        tiled=True,
    ).astype(jnp.float32)
    norm_sums = lax.psum(
        (attn_gain_part, attn_shift_part, final_gain_part, final_shift_part), ("dp", "mp")
    )
    summed = lax.psum(
        (
            grad_query_weight,
            grad_query_bias,
            grad_key_weight,
            grad_value_weight,
            grad_value_bias,
            grad_out_weight,
            grad_out_bias,
            grad_up_weight,
            grad_up_bias,
            grad_down_weight,
            grad_down_bias,
        ),
        "dp",
    )
    lower_grads = summed[:7]
    upper_grads = summed[7:]
    return (
        layer_out,
        grad_tokens,
        lower_grads[0],
        lower_grads[1],
        lower_grads[2],
        lower_grads[3],
        lower_grads[4],
        lower_grads[5],
        lower_grads[6],
        norm_sums[0],
        norm_sums[1],
        upper_grads[0],
        upper_grads[1],
        upper_grads[2],
        upper_grads[3],
        norm_sums[2],
        norm_sums[3],
    )


def solution(mesh):
    return jax.shard_map(
        body,
        mesh=mesh,
        in_specs=(
            P(("dp", "mp"), None),
            P("dp", None),
            P(),
            P("dp"),
            P(None, "mp"),
            P("mp"),
            P(None, "mp"),
            P(None, "mp"),
            P("mp"),
            P("mp", None),
            P(),
            P(),
            P(),
            P(None, "mp"),
            P("mp"),
            P("mp", None),
            P(),
            P(),
            P(),
            P(("dp", "mp"), None),
        ),
        out_specs=(
            P(("dp", "mp"), None),
            P(("dp", "mp"), None),
            P(None, "mp"),
            P("mp"),
            P(None, "mp"),
            P(None, "mp"),
            P("mp"),
            P("mp", None),
            P(),
            P(),
            P(),
            P(None, "mp"),
            P("mp"),
            P("mp", None),
            P(),
            P(),
            P(),
        ),
        check_vma=False,
    )
```

profile of v0, /device:TPU:0, one launch (start us, length us, event | category | flops | bytes accessed | tf_op | source)
XLA Modules:
  0.0 669.5 jit_solution(431593237311319448)
XLA Ops:
  9.6 29.3 %all-gather.5.cloned.1.call-done = bf16[1824,768]{1,0:T(8,128)(2,1)} async-done(((bf16[456,768]{1,0:T(8,128)(2,1)}), bf16[1824,768]{1,0:T(8,128)(2,1)}) %all-gather.5.cloned.1.call-update) | async-done | bytes 2801680 | tf_op jit(solution)/shard_map/all_gather | solution.py:107
  38.9 2.9 convolution_convert_fusion.1
  43.2 3.2 fusion.13
  47.7 4.1 fusion.12
  51.8 2.5 reshape.127
  54.4 1.8 fusion.43
  61.3 4.4 fusion.44
  65.8 53.7 %reduce-scatter.5.cloned.1.call-done = f32[456,768]{1,0:T(8,128)} async-done(((f32[1824,768]{1,0:T(8,128)}), f32[456,768]{1,0:T(8,128)}) %reduce-scatter.5.cloned.1.call-update) | async-done | bytes 1400848 | tf_op jit(solution)/shard_map/reduce_scatter | solution.py:116
  119.5 1.8 fusion.42
  123.3 26.2 %all-gather.7.cloned.1.call-done = bf16[1824,768]{1,0:T(8,128)(2,1)} async-done(((bf16[456,768]{1,0:T(8,128)(2,1)}), bf16[1824,768]{1,0:T(8,128)(2,1)}) %all-gather.7.cloned.1.call-update) | async-done | bytes 2801680 | tf_op jit(solution)/shard_map/all_gather | solution.py:129
  149.5 6.4 multiply_convert_fusion.1
  155.9 1.6 copy-done.39
  157.5 4.8 fusion.45
  162.4 53.8 %reduce-scatter.7.cloned.1.call-done = f32[456,768]{1,0:T(8,128)} async-done(((f32[1824,768]{1,0:T(8,128)}), f32[456,768]{1,0:T(8,128)}) %reduce-scatter.7.cloned.1.call-update) | async-done | bytes 1400848 | tf_op jit(solution)/shard_map/reduce_scatter | solution.py:133
  216.1 1.9 fusion.41
  220.6 26.7 %all-gather.9.cloned.1.call-done = bf16[1824,768]{1,0:T(8,128)(2,1)} async-done(((bf16[456,768]{1,0:T(8,128)(2,1)}), bf16[1824,768]{1,0:T(8,128)(2,1)}) %all-gather.9.cloned.1.call-update) | async-done | bytes 2801680 | tf_op jit(solution)/shard_map/all_gather | solution.py:192
  247.2 6.3 convert_reduce_fusion.1
  253.5 1.6 copy-done.40
  255.2 4.9 fusion.46
  260.1 53.8 %reduce-scatter.9.cloned.1.call-done = f32[456,768]{1,0:T(8,128)} async-done(((f32[1824,768]{1,0:T(8,128)}), f32[456,768]{1,0:T(8,128)}) %reduce-scatter.9.cloned.1.call-update) | async-done | bytes 1400848 | tf_op jit(solution)/shard_map/reduce_scatter | solution.py:201
  313.9 3.8 multiply_reduce_fusion.1
  317.7 1.8 fusion.39
  319.7 26.4 %all-gather.11.cloned.1.call-done = bf16[1824,768]{1,0:T(8,128)(2,1)} async-done(((bf16[456,768]{1,0:T(8,128)(2,1)}), bf16[1824,768]{1,0:T(8,128)(2,1)}) %all-gather.11.cloned.1.call-update) | async-done | bytes 2801680 | tf_op jit(solution)/shard_map/all_gather | solution.py:225
  346.2 2.9 convolution_convert_fusion
  350.4 3.9 convert_reduce_fusion.4
  354.4 4.4 multiply_reduce_fusion
  360.3 1.9 fusion.26
  362.2 1.5 convert_reduce_fusion.5
  364.1 1.8 convert_element_type.144
  365.9 1.6 copy.74
  368.5 2.5 copy.77
  370.9 2.1 convert_element_type.140
  375.3 2.5 add_convert_fusion
  377.9 6.9 %fusion.51 = f32[768,768]{1,0:T(8,128)} fusion(bf16[1824,768]{1,0:T(8,128)(2,1)} %copy-done.39, bf16[1824,768]{1,0:T(8,128)(2,1)} %all-gather.9.cloned.1.call-done), kind=kOutput, calls=%fused_computation.101 | convolution fusion | flops 2151677952 | bytes 7962624 | tf_op jit(solution)/shard_map/rf,rd->fd/dot_general | solution.py:193
  384.8 4.1 fusion.50
  388.9 1.6 fusion.49
  391.0 1.6 convolution_bitcast_fusion
  392.7 1.6 convolution_bitcast_fusion.1
  394.3 1.6 convolution_bitcast_fusion.2
  395.9 2.4 convert_reduce_fusion
  398.3 41.6 %all-reduce = (f32[768]{0:T(1024)}, f32[768]{0:T(1024)}, f32[768]{0:T(1024)}, f32[768]{0:T(1024)}) all-reduce(f32[768]{0:T(1024)S(1)} %get-tuple-element.17, f32[768]{0:T(1024)S(1)} %get-tuple-element.22, f32[768]{0:T(1024)S(1)} %get-tuple-element.19, f32[768]{0:T(1024)S(1)} %get-tuple-element.24), channel_id=1, replica_groups=mesh['dp'=8,'mp'=4] {'dp','mp'}, use_global_device_ids=true, to_apply=%region_27.28 | all-reduce | flops 3072 | bytes 24576 | tf_op jit(solution)/shard_map/psum | solution.py:258
  440.0 2.3 convert_reduce_fusion.2
  442.3 39.6 %all-reduce.1 = (f32[192]{0:T(256)}, f32[192]{0:T(256)}, f32[768]{0:T(1024)}, f32[768]{0:T(1024)}, f32[768]{0:T(1024)}) all-reduce(f32[192]{0:T(256)S(1)} %reduce_sum.216, f32[192]{0:T(256)S(1)} %reduce_sum.218, f32[768]{0:T(1024)S(1)} %convert_reduce_fusion.2, ...), channel_id=1, replica_groups=mesh['dp'=8,'mp'=4] {'dp'}, use_global_device_ids=true, to_apply=%region_18.19 | all-reduce | flops 2688 | bytes 21504 | tf_op jit(solution)/shard_map/psum | solution.py:261
  482.0 2.3 convert_add_fusion
  484.3 168.9 %all-reduce.5.cloned.1.call-done = (f32[768,192]{0,1:T(8,128)}, f32[768,192]{0,1:T(8,128)}, f32[768,192]{0,1:T(8,128)}, f32[192,768]{1,0:T(8,128)}, f32[768,768]{1,0:T(8,128)}, /*index=5*/f32[768,768]{1,0:T(8,128)}) async-done(((f32[768,192]{0,1:T(8,128)}, f32[768,192]{0,1:T(8,128)}, f32[768,192]{0,1:T(8,128)}, f32[192,768]{1,0:T(8,128)}, f32[768,768]{1,0:T(8,128)}, /*index=5*/f32[768,768]{1,0:T(8,128)}), ...) | async-done | bytes 7077904 | tf_op jit(solution)/shard_map/psum | solution.py:261
  653.2 2.1 copy.119
  655.2 1.9 copy.120
  657.2 1.9 copy.121
  (140 shorter events, 25.6 us)
Async XLA Ops:
  7.2 142.3 %copy-start = (bf16[768,768]{1,0:T(8,128)(2,1)S(1)}, bf16[768,768]{1,0:T(8,128)(2,1)}, u32[]{:S(2)}) copy-start(bf16[768,768]{1,0:T(8,128)(2,1)} %param.33) | copy-start | bytes 3538948
  7.2 31.7 %all-gather.5.cloned.1.call-start = ((), (), s32[]{:S(2)}) async-start(), calls=%async_computation.4 | async-start | bytes 3502080 | tf_op jit(solution)/shard_map/all_gather | solution.py:107
  7.9 111.6 %reduce-scatter.5.cloned.1.call-start = ((), (), s32[]{:S(2)}) async-start(), calls=%async_computation.5 | async-start | bytes 7004160 | tf_op jit(solution)/shard_map/reduce_scatter | solution.py:116
  9.6 33.5 %copy-start.37 = (f32[192]{0:T(256)S(1)}, f32[192]{0:T(256)}, u32[]{:S(2)}) copy-start(f32[192]{0:T(256)} %param.25) | copy-start | bytes 2308
  43.1 11.2 %copy-start.6 = (bf16[8,228,3,64]{1,0,3,2:T(8,128)(2,1)}, bf16[8,228,3,64]{1,0,3,2:T(8,128)(2,1)S(1)}, u32[]{:S(2)}) copy-start(bf16[8,228,3,64]{1,0,3,2:T(8,128)(2,1)S(1)} %reshape.129) | copy-start | bytes 2101252
  43.1 4.6 copy-start.38
  47.7 6.6 copy-start.8
  54.3 2.8 copy-start.15
  56.2 2.5 copy-start.2
  56.2 2.5 copy-start.20
  65.7 53.8 %copy-start.31 = (f32[768]{0:T(1024)S(1)}, f32[768]{0:T(1024)}, u32[]{:S(2)}) copy-start(f32[768]{0:T(1024)} %param.30) | copy-start | bytes 9220
  65.7 55.9 %copy-start.28 = (f32[768]{0:T(1024)S(1)}, f32[768]{0:T(1024)}, u32[]{:S(2)}) copy-start(f32[768]{0:T(1024)} %param.31) | copy-start | bytes 9220
  65.7 55.9 %copy-start.30 = (f32[768]{0:T(1024)S(1)}, f32[768]{0:T(1024)}, u32[]{:S(2)}) copy-start(f32[768]{0:T(1024)} %param.32) | copy-start | bytes 9220
  65.7 83.8 %all-gather.7.cloned.1.call-start = ((), (), s32[]{:S(2)}) async-start(), calls=%async_computation.6 | async-start | bytes 3502080 | tf_op jit(solution)/shard_map/all_gather | solution.py:129
  121.3 28.2 %copy-start.36 = (f32[768]{0:T(1024)S(1)}, f32[768]{0:T(1024)}, u32[]{:S(2)}) copy-start(f32[768]{0:T(1024)} %param.34) | copy-start | bytes 9220
  122.8 93.3 %reduce-scatter.7.cloned.1.call-start = ((), (), s32[]{:S(2)}) async-start(), calls=%async_computation.7 | async-start | bytes 7004160 | tf_op jit(solution)/shard_map/reduce_scatter | solution.py:133
  149.5 7.9 %copy-start.35 = (bf16[768,768]{1,0:T(8,128)(2,1)S(1)}, bf16[768,768]{1,0:T(8,128)(2,1)}, u32[]{:S(2)}) copy-start(bf16[768,768]{1,0:T(8,128)(2,1)} %param.35) | copy-start | bytes 3538948
  155.9 1.6 copy-start.39
  162.3 53.8 %copy-start.33 = (f32[768]{0:T(1024)S(1)}, f32[768]{0:T(1024)}, u32[]{:S(2)}) copy-start(f32[768]{0:T(1024)} %param.36) | copy-start | bytes 9220
  162.3 56.1 %copy-start.29 = (f32[768]{0:T(1024)S(1)}, f32[768]{0:T(1024)}, u32[]{:S(2)}) copy-start(f32[768]{0:T(1024)} %param.37) | copy-start | bytes 9220
  162.3 84.9 %all-gather.9.cloned.1.call-start = ((), (), s32[]{:S(2)}) async-start(), calls=%async_computation.8 | async-start | bytes 3502080 | tf_op jit(solution)/shard_map/all_gather | solution.py:192
  216.1 2.3 copy-start.12
  220.5 93.4 %reduce-scatter.9.cloned.1.call-start = ((), (), s32[]{:S(2)}) async-start(), calls=%async_computation.9 | async-start | bytes 7004160 | tf_op jit(solution)/shard_map/reduce_scatter | solution.py:201
  253.5 1.6 copy-start.40
  260.0 53.8 %copy-start.13 = (bf16[456,768]{1,0:T(8,128)(2,1)S(1)}, bf16[456,768]{1,0:T(8,128)(2,1)}, u32[]{:S(2)}) copy-start(bf16[456,768]{1,0:T(8,128)(2,1)} %param.39) | copy-start | bytes 2101252
  260.0 53.8 %copy-start.32 = (f32[768]{0:T(1024)S(1)}, f32[768]{0:T(1024)}, u32[]{:S(2)}) copy-start(f32[768]{0:T(1024)} %param.38) | copy-start | bytes 9220
  260.1 86.1 %all-gather.11.cloned.1.call-start = ((), (), s32[]{:S(2)}) async-start(), calls=%async_computation.10 | async-start | bytes 3502080 | tf_op jit(solution)/shard_map/all_gather | solution.py:225
  317.7 2.0 copy-start.21
  317.7 2.0 copy-start.27
  317.7 28.5 %copy-start.22 = (bf16[192,768]{1,0:T(8,128)(2,1)S(1)}, bf16[192,768]{1,0:T(8,128)(2,1)}, u32[]{:S(2)}) copy-start(bf16[192,768]{1,0:T(8,128)(2,1)} %param.29) | copy-start | bytes 884740
  319.5 162.5 %reduce-scatter.11.cloned.1.call-start = ((), (), s32[]{:S(2)}) async-start(), calls=%async_computation.11 | async-start | bytes 3502080 | tf_op jit(solution)/shard_map/reduce_scatter | solution.py:249
  350.4 4.0 copy-start.16
  350.4 8.4 %slice-start = ((s8[5701632]{0:T(1024)(128)(4,1)}), s8[4194304]{0:T(1024)(128)(4,1)S(1)}, s32[]{:S(2)}) async-start(s8[5701632]{0:T(1024)(128)(4,1)} %bitcast.74), calls=%async_computation.13 | async-start | bytes 8388608
  354.4 4.5 slice-start.1
  358.9 1.4 copy-start.9
  360.3 1.9 copy-start.7
  365.9 7.1 %copy-start.23 = (bf16[768,192]{0,1:T(8,128)(2,1)S(1)}, bf16[768,192]{0,1:T(8,128)(2,1)}, u32[]{:S(2)}) copy-start(bf16[768,192]{0,1:T(8,128)(2,1)} %param.24) | copy-start | bytes 884740
  377.8 275.3 %all-reduce.5.cloned.1.call-start = ((), (), s32[]{:S(2)}) async-start(), calls=%async_computation.12 | async-start | bytes 14155776 | tf_op jit(solution)/shard_map/psum | solution.py:261
  377.9 6.9 %copy-start.34 = (bf16[1824,768]{1,0:T(8,128)(2,1)S(1)}, bf16[1824,768]{1,0:T(8,128)(2,1)}, u32[]{:S(2)}) copy-start(bf16[1824,768]{1,0:T(8,128)(2,1)} %all-gather.7.cloned.1.call-done) | copy-start | bytes 8404996
  377.9 6.9 %copy-start.41 = (bf16[1824,768]{1,0:T(8,128)(2,1)S(1)}, bf16[1824,768]{1,0:T(8,128)(2,1)}, u32[]{:S(2)}) copy-start(bf16[1824,768]{1,0:T(8,128)(2,1)} %copy-done.40) | copy-start | bytes 8404996
  384.8 4.1 copy-start.5
  388.9 1.8 copy-start.4
  388.9 2.2 copy-start.11
  395.9 86.1 %copy-start.14 = (f32[456,768]{1,0:T(8,128)S(1)}, f32[456,768]{1,0:T(8,128)}, u32[]{:S(2)}) copy-start(f32[456,768]{1,0:T(8,128)} %get-tuple-element.41) | copy-start | bytes 4202500
  653.2 5.9 copy-start.19
  653.2 6.7 %copy-start.18 = (f32[768,768]{1,0:T(8,128)S(1)}, f32[768,768]{1,0:T(8,128)}, u32[]{:S(2)}) copy-start(f32[768,768]{1,0:T(8,128)} %get-tuple-element.73) | copy-start | bytes 7077892
  659.1 2.2 copy-start.17
  659.9 2.8 copy-start.1
  (5 other events, 5.6 us)
Sparse Core Ops, SparseCore 0:
  9.6 29.2 all-gather.4
  65.8 53.6 reduce-scatter.4
  122.9 26.5 all-gather.6
  162.4 53.6 reduce-scatter.6
  220.6 26.5 all-gather.8
  260.2 53.6 reduce-scatter.8
  319.6 26.5 all-gather.10
  377.9 36.2 reduce-scatter.10
  420.5 232.6 all-reduce.4
where the time goes:
time: 678 us; the launch traced here: 669 us
  waiting for transfers between devices  440 us (65%)
  blocking collectives  81.2 us (12%)
  matrix products  76.6 us (11%)
  local copies, waits for them, and re-layouts  32.5 us (5%)
  other arithmetic  24 us (4%)
  between operations  14.7 us (2%)
    psum x1, waiting for transfers between devices, body(): lax.psum((grad_query_weight, grad_query_bias, grad_key_weight, grad_value...  169 us
    reduce_scatter x1, waiting for transfers between devices, body(): lax.psum_scatter(jnp.einsum('rf,df->rd', grad_in, up_weight, preferred_el...  53.8 us
    reduce_scatter x1, waiting for transfers between devices, feedforward(): lax.psum_scatter(jnp.dot(act, down_weight, preferred_element_type=jnp.flo...  53.8 us
    reduce_scatter x1, waiting for transfers between devices, attention_forward(): lax.psum_scatter(jnp.dot(context, out_weight, preferred_element_type=jnp....  53.7 us
    psum x1, blocking collectives, body(): lax.psum((attn_gain_part, attn_shift_part, final_gain_part, final_shift_p...  41.6 us
    psum x1, blocking collectives, body(): lax.psum((grad_query_weight, grad_query_bias, grad_key_weight, grad_value...  39.6 us
    all_gather x1, waiting for transfers between devices, attention_forward(): whole = lax.all_gather(tokens, 'mp', axis=0, tiled=True)  29.3 us
    all_gather x1, waiting for transfers between devices, body(): lax.all_gather(grad_final.astype(jnp.bfloat16), 'mp', axis=0, tiled=True)  26.7 us
  transfers between devices with their start and end apart: 9, of which 8 were waited for; matrix products, arithmetic and copies ran while one was open for 4% of the time, Pallas kernels for 0%

commit v1 on v0

--- a/solution.py
+++ b/solution.py
@@ -104,7 +104,25 @@
     attn_gain,
     attn_shift,
 ):
-    whole = lax.all_gather(tokens, "mp", axis=0, tiled=True)
+    z1, row_out, val2 = (jax.lax.axis_size("mp"), jax.lax.axis_index("mp"), tokens.shape[0])
+    ledger = []
+    for idx in range(z1):
+        ledger.append((idx, (idx + 1) % z1))
+    windows = []
+    for idx in range(z1):
+        windows.append((idx, (idx - 1) % z1))
+    whole = jnp.zeros((*tokens.shape[:0], z1 * val2, *tokens.shape[1:]), tokens.dtype)
+    whole = lax.dynamic_update_slice_in_dim(whole, tokens, row_out * val2, axis=0)
+    s_next = carry_out = tokens
+    placed = z1 // 2
+    for m in range(1, placed + 1):
+        s_next = jax.lax.ppermute(s_next, "mp", ledger)
+        whole = lax.dynamic_update_slice_in_dim(whole, s_next, (row_out - m) % z1 * val2, axis=0)
+        if m < z1 - placed:
+            carry_out = jax.lax.ppermute(carry_out, "mp", windows)
+            whole = lax.dynamic_update_slice_in_dim(
+                whole, carry_out, (row_out + m) % z1 * val2, axis=0
+            )
     query = (jnp.dot(whole, query_weight, preferred_element_type=jnp.float32) + query_bias).astype(
         jnp.bfloat16
     )

time: 678 us -> 678 us (level)
  waiting for transfers between devices: 440 us -> 433 us
    all_gather x1 -> x0, waiting for transfers between devices: 29.3 us -> none  [attention_forward(): whole = lax.all_gather(tokens, 'mp', axis=0, tiled=True)]
    ppermute x0 -> x3, waiting for transfers between devices: none -> 19.7 us  [the longest x2 19.7 us: attention_forward(): s_next = jax.lax.ppermute(s_next, 'mp', ledger)]
    unnamed x94 -> x100, local copies, waits for them, and re-layouts: 15.2 us -> 16.4 us
  transfers between devices with their start and end apart: 9 -> 11, of which waited for: 8 -> 9; matrix products, arithmetic and copies ran while one was open for 4% -> 4% of each run, Pallas kernels for 0% -> 0%
where the time goes in v1:
time: 678 us; the launch traced here: 669 us
  waiting for transfers between devices  433 us (64%)
  blocking collectives  81.4 us (12%)
  matrix products  74.9 us (11%)
  local copies, waits for them, and re-layouts  34.1 us (5%)
  other arithmetic  24 us (4%)
  between operations  15 us (2%)
    psum x1, waiting for transfers between devices, body(): lax.psum((grad_query_weight, grad_query_bias, grad_key_weight, grad_value...  169 us
    reduce_scatter x1, waiting for transfers between devices, attention_forward(): lax.psum_scatter(jnp.dot(context, out_weight, preferred_element_type=jnp....  57.6 us
    reduce_scatter x1, waiting for transfers between devices, body(): lax.psum_scatter(jnp.einsum('rf,df->rd', grad_in, up_weight, preferred_el...  53.8 us
    reduce_scatter x1, waiting for transfers between devices, feedforward(): lax.psum_scatter(jnp.dot(act, down_weight, preferred_element_type=jnp.flo...  53.8 us
    psum x1, blocking collectives, body(): lax.psum((attn_gain_part, attn_shift_part, final_gain_part, final_shift_p...  41.8 us
    psum x1, blocking collectives, body(): lax.psum((grad_query_weight, grad_query_bias, grad_key_weight, grad_value...  39.5 us
    all_gather x1, waiting for transfers between devices, body(): lax.all_gather(grad_final.astype(jnp.bfloat16), 'mp', axis=0, tiled=True)  26.7 us
    all_gather x1, waiting for transfers between devices, body(): lax.all_gather(grad_first.astype(jnp.bfloat16), 'mp', axis=0, tiled=True)  26.4 us
  transfers between devices with their start and end apart: 11, of which 9 were waited for; matrix products, arithmetic and copies ran while one was open for 4% of the time, Pallas kernels for 0%

profile of v1, /device:TPU:0, one launch (start us, length us, event | category | flops | bytes accessed | tf_op | source)
XLA Modules:
  0.0 668.7 jit_solution(8141649928214548566)
XLA Ops:
  7.8 2.0 collective-permute-start.1
  11.3 12.3 %collective-permute-done = bf16[456,768]{1,0:T(8,128)(2,1)S(1)} collective-permute-done((bf16[456,768]{1,0:T(8,128)(2,1)}, bf16[456,768]{1,0:T(8,128)(2,1)S(1)}, u32[]{:S(2)}, u32[]{:S(2)}) %collective-permute-start) | collective-permute-done | bytes 700448 | tf_op jit(solution)/shard_map/ppermute | solution.py:119
  23.6 2.6 collective-permute-start.2
  26.6 7.4 %collective-permute-done.2 = bf16[456,768]{1,0:T(8,128)(2,1)S(1)} collective-permute-done((bf16[456,768]{1,0:T(8,128)(2,1)S(1)}, bf16[456,768]{1,0:T(8,128)(2,1)S(1)}, u32[]{:S(2)}, u32[]{:S(2)}) %collective-permute-start.2) | collective-permute-done | bytes 700448 | tf_op jit(solution)/shard_map/ppermute | solution.py:119
  38.2 3.2 fusion.13
  42.7 4.1 fusion.12
  46.8 2.5 reshape.127
  49.4 1.8 fusion.43
  56.3 4.4 fusion.44
  60.8 57.6 %reduce-scatter.5.cloned.1.call-done = f32[456,768]{1,0:T(8,128)} async-done(((f32[1824,768]{1,0:T(8,128)}), f32[456,768]{1,0:T(8,128)}) %reduce-scatter.5.cloned.1.call-update) | async-done | bytes 1400848 | tf_op jit(solution)/shard_map/reduce_scatter | solution.py:134
  118.4 1.8 fusion.42
  122.2 26.2 %all-gather.4.cloned.1.call-done = bf16[1824,768]{1,0:T(8,128)(2,1)} async-done(((bf16[456,768]{1,0:T(8,128)(2,1)}), bf16[1824,768]{1,0:T(8,128)(2,1)}) %all-gather.4.cloned.1.call-update) | async-done | bytes 2801680 | tf_op jit(solution)/shard_map/all_gather | solution.py:147
  148.4 6.4 multiply_convert_fusion.1
  156.3 4.8 fusion.45
  161.2 53.8 %reduce-scatter.7.cloned.1.call-done = f32[456,768]{1,0:T(8,128)} async-done(((f32[1824,768]{1,0:T(8,128)}), f32[456,768]{1,0:T(8,128)}) %reduce-scatter.7.cloned.1.call-update) | async-done | bytes 1400848 | tf_op jit(solution)/shard_map/reduce_scatter | solution.py:151
  215.0 1.9 fusion.41
  219.4 26.7 %all-gather.6.cloned.1.call-done = bf16[1824,768]{1,0:T(8,128)(2,1)} async-done(((bf16[456,768]{1,0:T(8,128)(2,1)}), bf16[1824,768]{1,0:T(8,128)(2,1)}) %all-gather.6.cloned.1.call-update) | async-done | bytes 2801680 | tf_op jit(solution)/shard_map/all_gather | solution.py:210
  246.1 6.3 convert_reduce_fusion.1
  252.4 1.6 copy-done.43
  254.0 4.9 fusion.46
  259.0 53.8 %reduce-scatter.9.cloned.1.call-done = f32[456,768]{1,0:T(8,128)} async-done(((f32[1824,768]{1,0:T(8,128)}), f32[456,768]{1,0:T(8,128)}) %reduce-scatter.9.cloned.1.call-update) | async-done | bytes 1400848 | tf_op jit(solution)/shard_map/reduce_scatter | solution.py:219
  312.8 3.8 multiply_reduce_fusion.1
  316.6 1.8 fusion.39
  318.6 26.4 %all-gather.8.cloned.1.call-done = bf16[1824,768]{1,0:T(8,128)(2,1)} async-done(((bf16[456,768]{1,0:T(8,128)(2,1)}), bf16[1824,768]{1,0:T(8,128)(2,1)}) %all-gather.8.cloned.1.call-update) | async-done | bytes 2801680 | tf_op jit(solution)/shard_map/all_gather | solution.py:243
  345.1 2.9 convolution_convert_fusion
  349.3 3.9 convert_reduce_fusion.4
  353.3 4.4 multiply_reduce_fusion
  359.2 1.9 fusion.26
  363.0 1.8 convert_element_type.144
  364.8 1.6 copy.74
  367.4 2.5 copy.77
  369.8 2.1 convert_element_type.140
  374.2 2.5 add_convert_fusion
  376.8 6.9 %fusion.51 = f32[768,768]{1,0:T(8,128)} fusion(bf16[1824,768]{1,0:T(8,128)(2,1)} %copy-done.42, bf16[1824,768]{1,0:T(8,128)(2,1)} %all-gather.6.cloned.1.call-done), kind=kOutput, calls=%fused_computation.102 | convolution fusion | flops 2151677952 | bytes 7962624 | tf_op jit(solution)/shard_map/rf,rd->fd/dot_general | solution.py:211
  383.7 4.1 fusion.50
  387.8 1.6 fusion.54
  389.4 1.6 fusion.53
  391.0 1.6 fusion.52
  392.8 1.6 fusion.49
  394.5 2.4 convert_reduce_fusion
  396.9 41.8 %all-reduce = (f32[768]{0:T(1024)}, f32[768]{0:T(1024)}, f32[768]{0:T(1024)}, f32[768]{0:T(1024)}) all-reduce(f32[768]{0:T(1024)S(1)} %get-tuple-element.17, f32[768]{0:T(1024)S(1)} %get-tuple-element.22, f32[768]{0:T(1024)S(1)} %get-tuple-element.19, f32[768]{0:T(1024)S(1)} %get-tuple-element.24), channel_id=1, replica_groups=mesh['dp'=8,'mp'=4] {'dp','mp'}, use_global_device_ids=true, to_apply=%region_27.28 | all-reduce | flops 3072 | bytes 24576 | tf_op jit(solution)/shard_map/psum | solution.py:276
  438.8 2.3 convert_reduce_fusion.2
  441.2 39.5 %all-reduce.1 = (f32[192]{0:T(256)}, f32[192]{0:T(256)}, f32[768]{0:T(1024)}, f32[768]{0:T(1024)}, f32[768]{0:T(1024)}) all-reduce(f32[192]{0:T(256)S(1)} %reduce_sum.216, f32[192]{0:T(256)S(1)} %reduce_sum.218, f32[768]{0:T(1024)S(1)} %convert_reduce_fusion.2, ...), channel_id=1, replica_groups=mesh['dp'=8,'mp'=4] {'dp'}, use_global_device_ids=true, to_apply=%region_18.19 | all-reduce | flops 2688 | bytes 21504 | tf_op jit(solution)/shard_map/psum | solution.py:279
  480.7 2.3 convert_add_fusion
  483.0 169.1 %all-reduce.5.cloned.1.call-done = (f32[768,192]{0,1:T(8,128)}, f32[768,192]{0,1:T(8,128)}, f32[768,192]{0,1:T(8,128)}, f32[192,768]{1,0:T(8,128)}, f32[768,768]{1,0:T(8,128)}, /*index=5*/f32[768,768]{1,0:T(8,128)}) async-done(((f32[768,192]{0,1:T(8,128)}, f32[768,192]{0,1:T(8,128)}, f32[768,192]{0,1:T(8,128)}, f32[192,768]{1,0:T(8,128)}, f32[768,768]{1,0:T(8,128)}, /*index=5*/f32[768,768]{1,0:T(8,128)}), ...) | async-done | bytes 7077904 | tf_op jit(solution)/shard_map/psum | solution.py:279
  652.1 2.1 copy.123
  654.2 1.9 copy.124
  656.1 1.9 copy.125
  (154 shorter events, 31.2 us)
Async XLA Ops:
  7.2 141.2 %copy-start = (bf16[768,768]{1,0:T(8,128)(2,1)S(1)}, bf16[768,768]{1,0:T(8,128)(2,1)}, u32[]{:S(2)}) copy-start(bf16[768,768]{1,0:T(8,128)(2,1)} %param.33) | copy-start | bytes 3538948
  7.2 19.2 %copy-start.18 = (bf16[456,768]{1,0:T(8,128)(2,1)S(1)}, bf16[456,768]{1,0:T(8,128)(2,1)}, u32[]{:S(2)}) copy-start(bf16[456,768]{1,0:T(8,128)(2,1)} %param.20) | copy-start | bytes 2101252
  7.2 111.2 %reduce-scatter.5.cloned.1.call-start = ((), (), s32[]{:S(2)}) async-start(), calls=%async_computation.4 | async-start | bytes 7004160 | tf_op jit(solution)/shard_map/reduce_scatter | solution.py:134
  7.3 16.3 %collective-permute-start = (bf16[456,768]{1,0:T(8,128)(2,1)}, bf16[456,768]{1,0:T(8,128)(2,1)S(1)}, u32[]{:S(2)}, u32[]{:S(2)}) collective-permute-start(bf16[456,768]{1,0:T(8,128)(2,1)} %param.20), channel_id=1, source_target_pairs={{0,1},{1,2},{2,3},{3,0},{4,5},{5,6},{6,7},{7,4},{8,9},{9,10},{10,1... | collective-permute-start | bytes 2101256 | tf_op jit(solution)/shard_map/ppermute | solution.py:119
  7.8 18.8 %collective-permute-start.1 = (bf16[456,768]{1,0:T(8,128)(2,1)}, bf16[456,768]{1,0:T(8,128)(2,1)S(1)}, u32[]{:S(2)}, u32[]{:S(2)}) collective-permute-start(bf16[456,768]{1,0:T(8,128)(2,1)} %param.20), channel_id=1, source_target_pairs={{0,3},{1,0},{2,1},{3,2},{4,7},{5,4},{6,5},{7,6},{8,11},{9,8},{10,9... | collective-permute-start | bytes 2101256 | tf_op jit(solution)/shard_map/ppermute | solution.py:122
  23.6 10.5 %collective-permute-start.2 = (bf16[456,768]{1,0:T(8,128)(2,1)S(1)}, bf16[456,768]{1,0:T(8,128)(2,1)S(1)}, u32[]{:S(2)}, u32[]{:S(2)}) collective-permute-start(bf16[456,768]{1,0:T(8,128)(2,1)S(1)} %collective-permute-done), channel_id=1, source_target_pairs={{0,1},{1,2},{2,3},{3,0},{4,5},{5,6},{6,7},{7,4},{8,9},{9,10},{10,1... | collective-permute-start | bytes 2101256 | tf_op jit(solution)/shard_map/ppermute | solution.py:119
  26.4 9.3 %copy-start.26 = (bf16[768,192]{0,1:T(8,128)(2,1)S(1)}, bf16[768,192]{0,1:T(8,128)(2,1)}, u32[]{:S(2)}) copy-start(bf16[768,192]{0,1:T(8,128)(2,1)} %param.26) | copy-start | bytes 884740
  35.7 2.4 copy-start.40
  38.2 11.2 %copy-start.7 = (bf16[8,228,3,64]{1,0,3,2:T(8,128)(2,1)}, bf16[8,228,3,64]{1,0,3,2:T(8,128)(2,1)S(1)}, u32[]{:S(2)}) copy-start(bf16[8,228,3,64]{1,0,3,2:T(8,128)(2,1)S(1)} %reshape.129) | copy-start | bytes 2101252
  38.2 4.5 copy-start.41
  42.7 6.6 copy-start.9
  49.4 2.8 copy-start.16
  51.2 2.5 copy-start.2
  51.2 2.5 copy-start.22
  60.7 57.7 %copy-start.34 = (f32[768]{0:T(1024)S(1)}, f32[768]{0:T(1024)}, u32[]{:S(2)}) copy-start(f32[768]{0:T(1024)} %param.30) | copy-start | bytes 9220
  60.7 59.7 %copy-start.31 = (f32[768]{0:T(1024)S(1)}, f32[768]{0:T(1024)}, u32[]{:S(2)}) copy-start(f32[768]{0:T(1024)} %param.31) | copy-start | bytes 9220
  60.8 59.7 %copy-start.33 = (f32[768]{0:T(1024)S(1)}, f32[768]{0:T(1024)}, u32[]{:S(2)}) copy-start(f32[768]{0:T(1024)} %param.32) | copy-start | bytes 9220
  60.8 87.6 %all-gather.4.cloned.1.call-start = ((), (), s32[]{:S(2)}) async-start(), calls=%async_computation.5 | async-start | bytes 3502080 | tf_op jit(solution)/shard_map/all_gather | solution.py:147
  120.2 28.2 %copy-start.39 = (f32[768]{0:T(1024)S(1)}, f32[768]{0:T(1024)}, u32[]{:S(2)}) copy-start(f32[768]{0:T(1024)} %param.34) | copy-start | bytes 9220
  121.7 93.3 %reduce-scatter.7.cloned.1.call-start = ((), (), s32[]{:S(2)}) async-start(), calls=%async_computation.6 | async-start | bytes 7004160 | tf_op jit(solution)/shard_map/reduce_scatter | solution.py:151
  148.4 7.9 %copy-start.38 = (bf16[768,768]{1,0:T(8,128)(2,1)S(1)}, bf16[768,768]{1,0:T(8,128)(2,1)}, u32[]{:S(2)}) copy-start(bf16[768,768]{1,0:T(8,128)(2,1)} %param.35) | copy-start | bytes 3538948
  161.1 53.8 %copy-start.36 = (f32[768]{0:T(1024)S(1)}, f32[768]{0:T(1024)}, u32[]{:S(2)}) copy-start(f32[768]{0:T(1024)} %param.36) | copy-start | bytes 9220
  161.2 56.1 %copy-start.32 = (f32[768]{0:T(1024)S(1)}, f32[768]{0:T(1024)}, u32[]{:S(2)}) copy-start(f32[768]{0:T(1024)} %param.37) | copy-start | bytes 9220
  161.2 84.9 %all-gather.6.cloned.1.call-start = ((), (), s32[]{:S(2)}) async-start(), calls=%async_computation.7 | async-start | bytes 3502080 | tf_op jit(solution)/shard_map/all_gather | solution.py:210
  215.0 2.3 copy-start.13
  219.4 93.4 %reduce-scatter.9.cloned.1.call-start = ((), (), s32[]{:S(2)}) async-start(), calls=%async_computation.8 | async-start | bytes 7004160 | tf_op jit(solution)/shard_map/reduce_scatter | solution.py:219
  258.9 53.8 %copy-start.14 = (bf16[456,768]{1,0:T(8,128)(2,1)S(1)}, bf16[456,768]{1,0:T(8,128)(2,1)}, u32[]{:S(2)}) copy-start(bf16[456,768]{1,0:T(8,128)(2,1)} %param.39) | copy-start | bytes 2101252
  258.9 53.8 %copy-start.35 = (f32[768]{0:T(1024)S(1)}, f32[768]{0:T(1024)}, u32[]{:S(2)}) copy-start(f32[768]{0:T(1024)} %param.38) | copy-start | bytes 9220
  259.0 86.1 %all-gather.8.cloned.1.call-start = ((), (), s32[]{:S(2)}) async-start(), calls=%async_computation.9 | async-start | bytes 3502080 | tf_op jit(solution)/shard_map/all_gather | solution.py:243
  316.6 2.0 copy-start.23
  316.6 2.0 copy-start.30
  316.6 28.5 %copy-start.24 = (bf16[192,768]{1,0:T(8,128)(2,1)S(1)}, bf16[192,768]{1,0:T(8,128)(2,1)}, u32[]{:S(2)}) copy-start(bf16[192,768]{1,0:T(8,128)(2,1)} %param.29) | copy-start | bytes 884740
  318.4 162.3 %reduce-scatter.11.cloned.1.call-start = ((), (), s32[]{:S(2)}) async-start(), calls=%async_computation.10 | async-start | bytes 3502080 | tf_op jit(solution)/shard_map/reduce_scatter | solution.py:267
  349.3 4.0 copy-start.17
  349.3 8.4 %slice-start = ((s8[5701632]{0:T(1024)(128)(4,1)}), s8[4194304]{0:T(1024)(128)(4,1)S(1)}, s32[]{:S(2)}) async-start(s8[5701632]{0:T(1024)(128)(4,1)} %bitcast.68), calls=%async_computation.12 | async-start | bytes 8388608
  353.3 4.5 slice-start.1
  359.2 1.9 copy-start.8
  364.8 7.1 %copy-start.25 = (bf16[768,192]{0,1:T(8,128)(2,1)S(1)}, bf16[768,192]{0,1:T(8,128)(2,1)}, u32[]{:S(2)}) copy-start(bf16[768,192]{0,1:T(8,128)(2,1)} %param.24) | copy-start | bytes 884740
  376.7 275.4 %all-reduce.5.cloned.1.call-start = ((), (), s32[]{:S(2)}) async-start(), calls=%async_computation.11 | async-start | bytes 14155776 | tf_op jit(solution)/shard_map/psum | solution.py:279
  376.8 6.9 %copy-start.37 = (bf16[1824,768]{1,0:T(8,128)(2,1)S(1)}, bf16[1824,768]{1,0:T(8,128)(2,1)}, u32[]{:S(2)}) copy-start(bf16[1824,768]{1,0:T(8,128)(2,1)} %all-gather.4.cloned.1.call-done) | copy-start | bytes 8404996
  376.8 6.9 %copy-start.44 = (bf16[1824,768]{1,0:T(8,128)(2,1)S(1)}, bf16[1824,768]{1,0:T(8,128)(2,1)}, u32[]{:S(2)}) copy-start(bf16[1824,768]{1,0:T(8,128)(2,1)} %copy-done.43) | copy-start | bytes 8404996
  383.7 4.1 copy-start.4
  383.7 4.1 copy-start.12
  394.5 86.2 %copy-start.15 = (f32[456,768]{1,0:T(8,128)S(1)}, f32[456,768]{1,0:T(8,128)}, u32[]{:S(2)}) copy-start(f32[456,768]{1,0:T(8,128)} %get-tuple-element.41) | copy-start | bytes 4202500
  652.1 5.9 copy-start.21
  652.1 6.7 %copy-start.20 = (f32[768,768]{1,0:T(8,128)S(1)}, f32[768,768]{1,0:T(8,128)}, u32[]{:S(2)}) copy-start(f32[768,768]{1,0:T(8,128)} %get-tuple-element.73) | copy-start | bytes 7077892
  658.0 2.2 copy-start.19
  658.8 2.8 copy-start.1
  (10 other events, 13.5 us)
Sparse Core Ops, SparseCore 0:
  60.9 57.4 reduce-scatter.4
  121.8 26.5 all-gather.3
  161.3 53.6 reduce-scatter.6
  219.5 26.5 all-gather.5
  259.1 53.6 reduce-scatter.8
  318.5 26.5 all-gather.7
  376.9 36.2 reduce-scatter.10
  419.4 232.6 all-reduce.4
